TPU v7x, 512 devices: a whole 4x4x16 slice. The times are simulated.
512 devices in a mesh: dp: 4 (over y), expert: 32 (over z, core), tensor: 4 (over x).
Axes of the slice: x: 4, y: 4, z: 16, core: 2. Of those that a mesh axis runs over, the one named last changes fastest.
Arguments:
- tokens: bfloat16 [16384, 2048], P(('dp', 'expert')), may hold values from -6 to 6
- cotangent: bfloat16 [16384, 2048], P(('dp', 'expert')), may hold values from -6 to 6
- expert_ids: int32 [16384, 1], P(('dp', 'expert')), may hold values from 0 to 31; in each aligned block of 128 rows (0 to 127, 128 to 255, ...) at most 8 rows name the same one
- gate_weight: bfloat16 [32, 2048, 1408], P('expert', 'dp', 'tensor'), may hold values from -0.125 to 0.125
- up_weight: bfloat16 [32, 2048, 1408], P('expert', 'dp', 'tensor'), may hold values from -0.125 to 0.125
- down_weight: bfloat16 [32, 2048, 1408], P('expert', 'dp', 'tensor'), may hold values from -0.15625 to 0.15625
Outputs:
- grad_tokens: bfloat16 [16384, 2048], P(('dp', 'expert'), 'tensor')
- grad_gate: bfloat16 [32, 2048, 1408], P('expert', 'dp', 'tensor')
- grad_up: bfloat16 [32, 2048, 1408], P('expert', 'dp', 'tensor')
Inputs may be any that keep to these rules, and one draw needn't show every extreme that they name: `expert_ids`: among the 128 tokens of one block no expert id occurs more than 8 times, and in every draw some block holds some id exactly 8 times.
All inputs are finite; a program needn't handle non-finite values.
Results may differ from a plain program's by a relative error of at most 0.013.
Values may be sent and summed in bfloat16 or wider, within the bound.
A program may use at most 64 MiB of HBM per device.

v0:
```python
import jax
import jax.numpy as jnp
from jax import lax
from jax.sharding import PartitionSpec as P

CAP = 8


def bucket_matrix(expert_ids, expert_count, capacity):
    chosen = expert_ids[:, 0]
    columns = jnp.arange(expert_count, dtype=jnp.int32)
    onehot = (chosen[:, None] == columns[None, :]).astype(jnp.int32)
    earlier = jnp.cumsum(onehot, axis=0) - onehot
    position = jnp.sum(earlier * onehot, axis=1)
    target = chosen * capacity + position
    slot_rows = jnp.arange(expert_count * capacity, dtype=jnp.int32)
    return (slot_rows[:, None] == target[None, :]).astype(jnp.bfloat16)


def on_device(tokens, cotangent, expert_ids, gate_weight, up_weight, down_weight):
    owners = lax.axis_size("expert")
    shards = lax.axis_size("tensor")
    features = tokens.shape[1]
    part = features // shards
    local_experts = gate_weight.shape[0]
    expert_count = local_experts * owners
    slot_count = owners * CAP
    placer = bucket_matrix(expert_ids, expert_count, CAP)
    gate_full, down_full, up_full = (
        lax.all_gather(w, "dp", axis=1, tiled=True)[0]
        for w in (gate_weight, down_weight, up_weight)
    )
    start = lax.axis_index("tensor") * part
    mine = jnp.concatenate(
        [lax.dynamic_slice_in_dim(a, start, part, axis=1) for a in (tokens, cotangent)], axis=1
    )
    packed = jnp.dot(placer, mine, preferred_element_type=jnp.float32).astype(jnp.bfloat16)
    arrived = lax.all_to_all(
        packed.reshape(owners, CAP, 2 * part), "expert", split_axis=0, concat_axis=0, tiled=True
    ).reshape(slot_count, 2 * part)
    whole = lax.all_gather(arrived, "tensor", axis=0, tiled=False)
    inputs = jnp.concatenate([whole[t, :, :part] for t in range(shards)], axis=1)
    grads_in = jnp.concatenate([whole[t, :, part:] for t in range(shards)], axis=1)
    gate_act = jnp.dot(inputs, gate_full, preferred_element_type=jnp.float32)
    hidden_grad = jnp.dot(grads_in, down_full, preferred_element_type=jnp.float32)
    up_act = jnp.dot(inputs, up_full, preferred_element_type=jnp.float32)
    sigmoid_gate = jax.nn.sigmoid(gate_act)
    up_grad = (hidden_grad * gate_act * sigmoid_gate).astype(jnp.bfloat16)
    gate_grad = (
        hidden_grad * up_act * sigmoid_gate * (1.0 + gate_act * (1.0 - sigmoid_gate))
    ).astype(jnp.bfloat16)
    contract = (((1,), (1,)), ((), ()))
    partial_value = lax.dot_general(
        gate_grad, gate_full, contract, preferred_element_type=jnp.float32
    )
    partial_value = partial_value + lax.dot_general(
        up_grad, up_full, contract, preferred_element_type=jnp.float32
    )
    rows = (((0,), (0,)), ((), ()))
    gate_term = lax.dot_general(inputs, gate_grad, rows, preferred_element_type=jnp.float32)
    up_term = lax.dot_general(inputs, up_grad, rows, preferred_element_type=jnp.float32)
    summed = lax.psum_scatter(
        partial_value.astype(jnp.bfloat16), "tensor", scatter_dimension=1, tiled=True
    )
    grad_gate, grad_up = (
        lax.psum_scatter(term.astype(jnp.bfloat16), "dp", scatter_dimension=0, tiled=True)[None]
        for term in (gate_term, up_term)
    )
    returned = lax.all_to_all(
        summed.reshape(owners, CAP, part), "expert", split_axis=0, concat_axis=0, tiled=True
    ).reshape(slot_count, part)
    per_token = lax.dot_general(placer, returned, rows, preferred_element_type=jnp.float32)
    return (per_token.astype(jnp.bfloat16), grad_gate, grad_up)


def solution(mesh):
    placed = (
        P(("dp", "expert"), None),
        P(("dp", "expert"), None),
        P(("dp", "expert"), None),
        P("expert", "dp", "tensor"),
        P("expert", "dp", "tensor"),
        P("expert", "dp", "tensor"),
    )
    return jax.shard_map(
        on_device,
        mesh=mesh,
        in_specs=placed,
        out_specs=(
            P(("dp", "expert"), "tensor"),
            P("expert", "dp", "tensor"),
            P("expert", "dp", "tensor"),
        ),
        check_vma=False,
    )
```

profile of v0, /device:TPU:4, one launch (start us, length us, event | category | flops | bytes accessed | tf_op | source)
XLA Modules:
  0.0 313.7 jit_solution(8685269563842167810)
XLA Ops:
  7.2 0.0 all-gather.5.cloned.1.call-start
  7.2 0.7 fusion.36
  8.0 0.2 reduce_window_sum.11
  8.1 0.8 select_reduce_fusion
  9.0 0.7 multiply_add_fusion
  9.6 1.0 constant_dynamic-slice_fusion
  10.6 0.3 fusion.10
  10.9 49.1 %all_to_all.10 = bf16[32,8,1024]{2,1,0:T(8,128)(2,1)} all-to-all(bf16[32,8,1024]{2,1,0:T(8,128)(2,1)S(1)} %fusion.10), channel_id=1, replica_groups=mesh['dp'=4,'expert'=32,'tensor'=4] {'expert'}, dimensions={0} | all-to-all | bytes 1048576 | tf_op jit(solution)/shard_map/all_to_all | solution.py:38
  60.1 0.0 all-gather.11.cloned.1.call-start
  60.1 0.7 all-gather.11.cloned.1.call-update
  60.9 0.7 all-gather.7.cloned.1.call-update
  61.6 0.5 all-gather.9.cloned.1.call-update
  62.2 26.8 %all-gather.5.cloned.1.call-done = bf16[4,256,1024]{2,1,0:T(8,128)(2,1)} async-done(((bf16[1,256,1024]{2,1,0:T(8,128)(2,1)}), bf16[4,256,1024]{2,1,0:T(8,128)(2,1)}) %all-gather.5.cloned.1.call-update) | async-done | bytes 2097168 | tf_op jit(solution)/shard_map/all_gather | solution.py:41
  89.0 1.7 slice_bitcast_fusion.3
  90.7 34.9 %all-gather.11.cloned.1.call-done = bf16[1,2048,352]{1,2,0:T(8,128)(2,1)} async-done(((bf16[1,512,352]{1,2,0:T(8,128)(2,1)}), bf16[1,2048,352]{1,2,0:T(8,128)(2,1)}) %all-gather.11.cloned.1.call-update) | async-done | bytes 1441808 | tf_op jit(solution)/shard_map/all_gather | solution.py:30
  125.6 1.9 fusion.3
  127.5 33.9 %all-gather.7.cloned.1.call-done = bf16[1,2048,352]{1,2,0:T(8,128)(2,1)} async-done(((bf16[1,512,352]{1,2,0:T(8,128)(2,1)}), bf16[1,2048,352]{1,2,0:T(8,128)(2,1)}) %all-gather.7.cloned.1.call-update) | async-done | bytes 1441808 | tf_op jit(solution)/shard_map/all_gather | solution.py:30
  161.5 1.9 multiply_convert_fusion
  163.4 33.8 %all-gather.9.cloned.1.call-done = bf16[1,2048,352]{1,2,0:T(8,128)(2,1)} async-done(((bf16[1,512,352]{1,2,0:T(8,128)(2,1)}), bf16[1,2048,352]{1,2,0:T(8,128)(2,1)}) %all-gather.9.cloned.1.call-update) | async-done | bytes 1441808 | tf_op jit(solution)/shard_map/all_gather | solution.py:30
  197.2 2.1 fusion.20
  199.3 0.7 fusion.1
  200.0 0.6 copy-done.1
  200.7 1.7 fusion
  202.4 0.0 reduce-scatter.8.cloned.1.call-start
  202.4 1.6 convolution_convert_fusion
  204.1 0.0 reduce-scatter.6.cloned.1.call-start
  204.2 1.7 convolution_convert_fusion.1
  205.9 26.9 %reduce-scatter.4.cloned.1.call-done = bf16[256,512]{1,0:T(8,128)(2,1)} async-done(((bf16[256,2048]{1,0:T(8,128)(2,1)}), bf16[256,512]{1,0:T(8,128)(2,1)}) %reduce-scatter.4.cloned.1.call-update) | async-done | bytes 262160 | tf_op jit(solution)/shard_map/reduce_scatter | solution.py:62
  232.8 35.4 %all_to_all.11 = bf16[32,8,512]{2,1,0:T(8,128)(2,1)S(1)} all-to-all(bf16[32,8,512]{2,1,0:T(8,128)(2,1)} %bitcast.55), channel_id=1, replica_groups=mesh['dp'=4,'expert'=32,'tensor'=4] {'expert'}, dimensions={0} | all-to-all | bytes 524288 | tf_op jit(solution)/shard_map/all_to_all | solution.py:69
  268.2 0.9 convolution_convert_fusion.3
  269.0 1.5 reduce-scatter.8.cloned.1.call-done
  270.5 36.3 %reduce-scatter.6.cloned.1.call-done = bf16[512,352]{0,1:T(8,128)(2,1)} async-done(((bf16[2048,352]{0,1:T(8,128)(2,1)}), bf16[512,352]{0,1:T(8,128)(2,1)}) %reduce-scatter.6.cloned.1.call-update) | async-done | bytes 360464 | tf_op jit(solution)/shard_map/reduce_scatter | solution.py:66
  (10 shorter events, 0.2 us)
Async XLA Ops:
  7.2 81.8 %all-gather.5.cloned.1.call-start = ((), (), s32[]{:S(2)}) async-start(), calls=%async_computation.5 | async-start | bytes 2621440 | tf_op jit(solution)/shard_map/all_gather | solution.py:41
  60.1 65.5 %all-gather.11.cloned.1.call-start = ((), (), s32[]{:S(2)}) async-start(), calls=%async_computation.8 | async-start | bytes 1802240 | tf_op jit(solution)/shard_map/all_gather | solution.py:30
  60.8 100.6 %all-gather.7.cloned.1.call-start = ((), (), s32[]{:S(2)}) async-start(), calls=%async_computation.6 | async-start | bytes 1802240 | tf_op jit(solution)/shard_map/all_gather | solution.py:30
  61.6 135.6 %all-gather.9.cloned.1.call-start = ((), (), s32[]{:S(2)}) async-start(), calls=%async_computation.7 | async-start | bytes 1802240 | tf_op jit(solution)/shard_map/all_gather | solution.py:30
  62.1 170.6 %reduce-scatter.4.cloned.1.call-start = ((), (), s32[]{:S(2)}) async-start(), calls=%async_computation.9 | async-start | bytes 1310720 | tf_op jit(solution)/shard_map/reduce_scatter | solution.py:62
  197.2 2.1 copy-start
  199.3 1.4 copy-start.1
  202.4 68.1 %reduce-scatter.8.cloned.1.call-start = ((), (), s32[]{:S(2)}) async-start(), calls=%async_computation.11 | async-start | bytes 1802240 | tf_op jit(solution)/shard_map/reduce_scatter | solution.py:66
  204.1 102.7 %reduce-scatter.6.cloned.1.call-start = ((), (), s32[]{:S(2)}) async-start(), calls=%async_computation.10 | async-start | bytes 1802240 | tf_op jit(solution)/shard_map/reduce_scatter | solution.py:66
Sparse Core Ops, SparseCore 0:
  60.2 28.7 all-gather.4
  91.1 34.4 all-gather.10
  127.7 33.7 all-gather.6
  163.4 33.7 all-gather.8
  202.5 30.1 reduce-scatter.3
  236.3 34.1 reduce-scatter.7
  274.2 32.5 reduce-scatter.5
where the time goes:
time: 314 us
  waiting for transfers between devices  196 us (62%)
  blocking collectives  84.6 us (27%)
  between operations  14.2 us (5%)
  matrix products  12.9 us (4%)
  local copies, waits for them, and re-layouts  3.33 us (1%)
    all_gather x3, waiting for transfers between devices, on_device(): lax.all_gather(w, 'dp', axis=1, tiled=True)[0]  103 us
    all_to_all x1, blocking collectives, on_device(): lax.all_to_all(packed.reshape(owners, CAP, 2 * part), 'expert', split_axi...  49.1 us
    reduce_scatter x2, waiting for transfers between devices, on_device(): lax.psum_scatter(term.astype(jnp.bfloat16), 'dp', scatter_dimension=0, ti...  37.8 us
    all_to_all x1, blocking collectives, on_device(): lax.all_to_all(summed.reshape(owners, CAP, part), 'expert', split_axis=0,...  35.4 us
    reduce_scatter x1, waiting for transfers between devices, on_device(): lax.psum_scatter(partial_value.astype(jnp.bfloat16), 'tensor', scatter_di...  26.9 us
    all_gather x1, waiting for transfers between devices, on_device(): whole = lax.all_gather(arrived, 'tensor', axis=0, tiled=False)  26.8 us
  transfers between devices with their start and end apart: 7, of which 7 were waited for; matrix products, arithmetic and copies ran while one was open for 3% of the time, Pallas kernels for 0%

commit v1 on v0

--- a/solution.py
+++ b/solution.py
@@ -27,7 +27,7 @@
     slot_count = owners * CAP
     placer = bucket_matrix(expert_ids, expert_count, CAP)
     gate_full, down_full, up_full = (
-        lax.all_gather(w, "dp", axis=1, tiled=True)[0]
+        jnp.concatenate(lax.all_to_all(jnp.stack([w] * lax.axis_size("dp")), "dp", 0, 0), axis=1)[0]
         for w in (gate_weight, down_weight, up_weight)
     )
     start = lax.axis_index("tensor") * part

time: 314 us -> 241 us (0.77)
  the two profiles are of different devices: /device:TPU:4 before, /device:TPU:2 now
where the time goes in v1:
time: 241 us; the launch traced here: 240 us
  blocking collectives  106 us (44%)
  waiting for transfers between devices  86.6 us (36%)
  between operations  14 us (6%)
  local copies, waits for them, and re-layouts  12.8 us (5%)
  matrix products  9.63 us (4%)
  starting transfers between devices  8.27 us (3%)
  other arithmetic  2.45 us (1%)
    all_to_all x1, blocking collectives, on_device(): lax.all_to_all(packed.reshape(owners, CAP, 2 * part), 'expert', split_axi...  49.1 us
    reduce_scatter x2, waiting for transfers between devices, on_device(): lax.psum_scatter(term.astype(jnp.bfloat16), 'dp', scatter_dimension=0, ti...  38.1 us
    all_to_all x1, blocking collectives, on_device(): lax.all_to_all(summed.reshape(owners, CAP, part), 'expert', split_axis=0,...  35.4 us
    all_to_all x2, waiting for transfers between devices, on_device(): lax.all_to_all(jnp.stack([w] * lax.axis_size('dp')), 'dp', 0, 0)  31.3 us
    all_to_all x1, blocking collectives, on_device(): lax.all_to_all(jnp.stack([w] * lax.axis_size('dp')), 'dp', 0, 0)  21.8 us
    reduce_scatter x1, waiting for transfers between devices, on_device(): lax.psum_scatter(partial_value.astype(jnp.bfloat16), 'tensor', scatter_di...  16.5 us
    all_to_all x2, starting transfers between devices, on_device(): lax.all_to_all(jnp.stack([w] * lax.axis_size('dp')), 'dp', 0, 0)  8.15 us
  transfers between devices with their start and end apart: 6, of which 5 were waited for; matrix products, arithmetic and copies ran while one was open for 5% of the time, Pallas kernels for 0%

profile of v1, /device:TPU:2, one launch (start us, length us, event | category | flops | bytes accessed | tf_op | source)
XLA Modules:
  0.0 240.1 jit_solution(3201230682311457094)
XLA Ops:
  7.2 0.8 fusion.19
  8.1 0.8 select_reduce_fusion
  9.0 0.7 multiply_add_fusion
  9.6 1.0 constant_dynamic-slice_fusion
  10.9 49.1 %all_to_all.25 = bf16[32,8,1024]{2,1,0:T(8,128)(2,1)} all-to-all(bf16[32,8,1024]{2,1,0:T(8,128)(2,1)S(1)} %fusion.1), channel_id=1, replica_groups=mesh['dp'=4,'expert'=32,'tensor'=4] {'expert'}, dimensions={0} | all-to-all | bytes 1048576 | tf_op jit(solution)/shard_map/all_to_all | solution.py:38
  60.1 1.2 stack.8
  61.3 4.6 %all-to-all-start.3 = ((bf16[4,1,512,352]{2,3,1,0:T(8,128)(2,1)}), bf16[4,1,512,352]{2,3,1,0:T(8,128)(2,1)S(1)}, u32[]{:S(2)}, u32[]{:S(2)}) async-start(bf16[4,1,512,352]{2,3,1,0:T(8,128)(2,1)} %stack.8), calls=%async_computation.3 | async-start | bytes 2883584 | tf_op jit(solution)/shard_map/all_to_all | solution.py:30
  65.9 0.7 all-gather.2.cloned.1.call-update
  66.6 18.8 %all-to-all-done.3 = bf16[4,1,512,352]{2,3,1,0:T(8,128)(2,1)S(1)} async-done(((bf16[4,1,512,352]{2,3,1,0:T(8,128)(2,1)}), bf16[4,1,512,352]{2,3,1,0:T(8,128)(2,1)S(1)}, u32[]{:S(2)}, u32[]{:S(2)}) %all-to-all-start.3) | async-done | bytes 1441824 | tf_op jit(solution)/shard_map/all_to_all | solution.py:30
  85.5 21.8 %all_to_all.26 = bf16[4,1,512,352]{2,3,1,0:T(8,128)(2,1)} all-to-all(bf16[4,1,512,352]{2,3,1,0:T(8,128)(2,1)S(1)} %stack.6), channel_id=1, replica_groups=mesh['dp'=4,'expert'=32,'tensor'=4] {'dp'}, dimensions={0} | all-to-all | bytes 2883584 | tf_op jit(solution)/shard_map/all_to_all | solution.py:30
  107.3 1.2 stack.7
  108.5 3.5 %all-to-all-start.2 = ((bf16[4,1,512,352]{2,3,1,0:T(8,128)(2,1)}), bf16[4,1,512,352]{2,3,1,0:T(8,128)(2,1)S(1)}, u32[]{:S(2)}, u32[]{:S(2)}) async-start(bf16[4,1,512,352]{2,3,1,0:T(8,128)(2,1)} %stack.7), calls=%async_computation.2 | async-start | bytes 2883584 | tf_op jit(solution)/shard_map/all_to_all | solution.py:30
  112.1 1.1 copy.14
  113.7 1.0 copy-done
  114.6 1.1 copy.12
  115.7 1.5 copy.15
  117.2 12.5 %all-to-all-done.2 = bf16[4,1,512,352]{2,3,1,0:T(8,128)(2,1)S(1)} async-done(((bf16[4,1,512,352]{2,3,1,0:T(8,128)(2,1)}), bf16[4,1,512,352]{2,3,1,0:T(8,128)(2,1)S(1)}, u32[]{:S(2)}, u32[]{:S(2)}) %all-to-all-start.2) | async-done | bytes 1441824 | tf_op jit(solution)/shard_map/all_to_all | solution.py:30
  129.7 1.1 copy.13
  131.3 1.6 slice_bitcast_fusion.3
  133.0 0.6 fusion.22
  133.6 0.9 copy-done.1
  134.5 0.6 multiply_convert_fusion
  135.1 0.6 fusion.4
  135.7 0.7 fusion.23
  136.5 1.7 fusion
  138.3 2.6 %convolution_convert_fusion = bf16[2048,352]{0,1:T(8,128)(2,1)} fusion(bf16[256,352]{0,1:T(8,128)(2,1)} %copy-done.11, bf16[256,512]{1,0:T(8,128)(2,1)S(1)} %get-tuple-element.4, bf16[256,512]{1,0:T(8,128)(2,1)S(1)} %copy-done.6, bf16[256,512]{1,0:T(8,128)(2,1)S(1)} %copy-done.8, bf16[256,512]{1,0:T(8,128)(2,1)S(1)} %get-tuple-element.3), kind=kOutput, calls=%fused_computation | convolution fusion | flops 374013952 | bytes 2670592 | tf_op jit(solution)/shard_map/dot_general | solution.py:61
  141.0 1.7 convolution_convert_fusion.1
  142.7 16.5 %reduce-scatter.4.cloned.1.call-done = bf16[256,512]{1,0:T(8,128)(2,1)} async-done(((bf16[256,2048]{1,0:T(8,128)(2,1)}), bf16[256,512]{1,0:T(8,128)(2,1)}) %reduce-scatter.4.cloned.1.call-update) | async-done | bytes 262160 | tf_op jit(solution)/shard_map/reduce_scatter | solution.py:62
  159.2 35.4 %all_to_all.27 = bf16[32,8,512]{2,1,0:T(8,128)(2,1)S(1)} all-to-all(bf16[32,8,512]{2,1,0:T(8,128)(2,1)} %bitcast.66), channel_id=1, replica_groups=mesh['dp'=4,'expert'=32,'tensor'=4] {'expert'}, dimensions={0} | all-to-all | bytes 524288 | tf_op jit(solution)/shard_map/all_to_all | solution.py:69
  194.5 0.9 convolution_convert_fusion.3
  195.4 2.0 reduce-scatter.8.cloned.1.call-done
  197.4 36.1 %reduce-scatter.6.cloned.1.call-done = bf16[512,352]{0,1:T(8,128)(2,1)} async-done(((bf16[2048,352]{0,1:T(8,128)(2,1)}), bf16[512,352]{0,1:T(8,128)(2,1)}) %reduce-scatter.6.cloned.1.call-update) | async-done | bytes 360464 | tf_op jit(solution)/shard_map/reduce_scatter | solution.py:66
  (35 shorter events, 1.6 us)
Async XLA Ops:
  7.2 52.9 %copy-start.2 = (bf16[1,512,352]{1,2,0:T(8,128)(2,1)S(1)}, bf16[1,512,352]{1,2,0:T(8,128)(2,1)}, u32[]{:S(2)}) copy-start(bf16[1,512,352]{1,2,0:T(8,128)(2,1)} %param.9) | copy-start | bytes 1081348
  61.3 24.1 %copy-start.3 = (bf16[1,512,352]{1,2,0:T(8,128)(2,1)S(1)}, bf16[1,512,352]{1,2,0:T(8,128)(2,1)}, u32[]{:S(2)}) copy-start(bf16[1,512,352]{1,2,0:T(8,128)(2,1)} %param.11) | copy-start | bytes 1081348
  61.3 24.1 %all-to-all-start.3 = ((bf16[4,1,512,352]{2,3,1,0:T(8,128)(2,1)}), bf16[4,1,512,352]{2,3,1,0:T(8,128)(2,1)S(1)}, u32[]{:S(2)}, u32[]{:S(2)}) async-start(bf16[4,1,512,352]{2,3,1,0:T(8,128)(2,1)} %stack.8), calls=%async_computation.3 | async-start | bytes 2883584 | tf_op jit(solution)/shard_map/all_to_all | solution.py:30
  65.9 65.4 %all-gather.2.cloned.1.call-start = ((), (), s32[]{:S(2)}) async-start(), calls=%async_computation.8 | async-start | bytes 2621440 | tf_op jit(solution)/shard_map/all_gather | solution.py:41
  85.4 21.9 %copy-start.4 = (bf16[1,512,352]{1,2,0:T(8,128)(2,1)S(1)}, bf16[1,512,352]{1,2,0:T(8,128)(2,1)}, u32[]{:S(2)}) copy-start(bf16[1,512,352]{1,2,0:T(8,128)(2,1)} %param.10) | copy-start | bytes 1081348
  108.5 21.2 %all-to-all-start.2 = ((bf16[4,1,512,352]{2,3,1,0:T(8,128)(2,1)}), bf16[4,1,512,352]{2,3,1,0:T(8,128)(2,1)S(1)}, u32[]{:S(2)}, u32[]{:S(2)}) async-start(bf16[4,1,512,352]{2,3,1,0:T(8,128)(2,1)} %stack.7), calls=%async_computation.2 | async-start | bytes 2883584 | tf_op jit(solution)/shard_map/all_to_all | solution.py:30
  112.1 47.1 %reduce-scatter.4.cloned.1.call-start = ((), (), s32[]{:S(2)}) async-start(), calls=%async_computation.9 | async-start | bytes 1310720 | tf_op jit(solution)/shard_map/reduce_scatter | solution.py:62
  113.3 1.4 copy-start
  132.9 2.2 copy-start.5
  132.9 2.2 copy-start.7
  133.0 1.5 copy-start.1
  135.1 1.4 copy-start.11
  135.7 0.7 copy-start.9
  136.5 1.8 copy-start.6
  136.5 1.8 copy-start.8
  138.3 2.8 %copy-start.10 = (bf16[256,352]{0,1:T(8,128)(2,1)S(1)}, bf16[256,352]{0,1:T(8,128)(2,1)}, u32[]{:S(2)}) copy-start(bf16[256,352]{0,1:T(8,128)(2,1)} %copy-done.9) | copy-start | bytes 540676
  138.3 59.2 %reduce-scatter.8.cloned.1.call-start = ((), (), s32[]{:S(2)}) async-start(), calls=%async_computation.11 | async-start | bytes 1802240 | tf_op jit(solution)/shard_map/reduce_scatter | solution.py:66
  141.0 92.6 %reduce-scatter.6.cloned.1.call-start = ((), (), s32[]{:S(2)}) async-start(), calls=%async_computation.10 | async-start | bytes 1802240 | tf_op jit(solution)/shard_map/reduce_scatter | solution.py:66
Sparse Core Ops, SparseCore 0:
  68.8 29.3 all-gather.1
  138.4 20.7 reduce-scatter.3
  162.9 34.5 reduce-scatter.7
  201.0 32.5 reduce-scatter.5
